TPU v7x, 32 devices: a whole 2x2x4 slice. The times are simulated.
32 devices in a mesh: rows: 4 (over z), cols: 8 (over y, x, core).
Axes of the slice: x: 2, y: 2, z: 4, core: 2. Of those that a mesh axis runs over, the one named last changes fastest.
Arguments:
- left_query: bfloat16 [8, 1024, 256], P('rows', 'cols'), parts along dimension 0, may hold values from -16 to 16
- left_value: bfloat16 [8, 1024, 256], P('rows', 'cols'), parts along dimension 0, may hold values from -6 to 6
- right_key: bfloat16 [8, 1024, 256], P('rows', 'cols'), parts along dimension 0, may hold values from -16 to 16
- right_value: bfloat16 [8, 1024, 256], P('rows', 'cols'), parts along dimension 0, may hold values from -6 to 6
- bound: int32 [8], P('rows'), parts along dimension 0, may hold values from 0 to 7
Outputs:
- left_out: bfloat16 [8, 1024, 256], P('rows', 'cols'), parts along dimension 0
- right_out: bfloat16 [8, 1024, 256], P('rows', 'cols'), parts along dimension 0
There are 4 independent parts, one for each index of `rows`. A program takes and returns all parts, laid end to end along the dimension named above; each array names one. Nothing has to cross between parts.
All inputs are finite; a program needn't handle non-finite values.
Results may differ from a plain program's by a relative error of at most 0.0045.
Values may be sent and summed in bfloat16 or wider, within the bound.
No kernel may reach another device: no remote copies, remote signals or barrier semaphores. Data moves between devices by JAX's collectives and lax.ppermute only.
A program may use at most 64 MiB of HBM per device.

v0:
```python
import functools
import math

import jax
import jax.numpy as jnp
from jax import lax
from jax.experimental import pallas as pl
from jax.experimental.pallas import tpu as pltpu
from jax.sharding import PartitionSpec as P


LOW = -1e30
SMEM = pl.BlockSpec(memory_space=pltpu.SMEM)
VMEM = pl.BlockSpec(memory_space=pltpu.VMEM)


def scores(a, b, scale):
    return lax.dot_general(a, b, (((1,), (1,)), ((), ())), preferred_element_type=jnp.float32) * scale


def weighted(w, v):
    return jnp.dot(w.astype(jnp.bfloat16), v, preferred_element_type=jnp.float32)


def own_kernel(scale, bound_ref, q_ref, lv_ref, k_ref, rv_ref, mine, top, total, acc, bias):
    rows_n, width, _ = q_ref.shape
    here = lax.axis_index("cols")
    lane = lax.broadcasted_iota(jnp.int32, (width, width), 1)
    sub = lax.broadcasted_iota(jnp.int32, (width, width), 0)
    for other in range(bias.shape[0]):
        for r in range(rows_n):
            allowed = jnp.abs(other - here) <= bound_ref[r]
            bias[other, r] = jnp.full((1, width), jnp.where(allowed, 0.0, LOW), jnp.float32)
    for side, (a_ref, b_ref, v_ref) in enumerate(((q_ref, k_ref, rv_ref), (k_ref, q_ref, lv_ref))):
        valid = (lane <= sub) if side == 0 else (lane >= sub)
        for r in range(rows_n):
            mine[side, r] = a_ref[r]
            s = jnp.where(valid, scores(a_ref[r], b_ref[r], scale), LOW)
            m = jnp.max(s, axis=-1, keepdims=True)
            w = jnp.exp(s - m)
            top[side, r] = m
            total[side, r] = jnp.sum(w, axis=-1, keepdims=True)
            acc[side, r] = weighted(w, v_ref[r])


def source(even_step, odd_step):
    here = lax.axis_index("cols")
    return here ^ jnp.where(here % 2 == 1, odd_step, even_step)


def fold(scale, bias, mine, state, new_state, group):
    top, total, acc = state
    new_top, new_total, new_acc = new_state
    others = [source(*steps) for _, steps in group]
    side = (others[0] > lax.axis_index("cols")).astype(jnp.int32)
    for r in range(mine.shape[1]):
        own = mine[side, r]
        parts = [
            scores(own, piece[0, r], scale) + bias[other, r]
            for (piece, _), other in zip(group, others)
        ]
        old = top[side, r]
        m = old
        for s in parts:
            m = jnp.maximum(m, jnp.max(s, axis=-1, keepdims=True))
        factor = jnp.exp(old - m)
        summed = total[side, r] * factor
        product = acc[side, r] * factor
        for s, (piece, _) in zip(parts, group):
            w = jnp.exp(s - m)
            summed = summed + jnp.sum(w, axis=-1, keepdims=True)
            product = product + weighted(w, piece[1, r])
        new_top[side, r] = m
        new_total[side, r] = summed
        new_acc[side, r] = product


def fold_kernel(steps, scale, bias, mine, top, total, acc, *rest):
    pieces, outs = rest[: len(steps)], rest[len(steps) :]
    fold(scale, bias, mine, (top, total, acc), outs, list(zip(pieces, steps)))


def last_kernel(steps, scale, bias, mine, top, total, acc, *rest):
    pieces, (left_ref, right_ref) = rest[: len(steps)], rest[len(steps) :]
    state = (top, total, acc)
    fold(scale, bias, mine, state, state, list(zip(pieces, steps)))
    for side, out in enumerate((left_ref, right_ref)):
        for r in range(out.shape[0]):
            out[r] = (acc[side, r] / total[side, r]).astype(out.dtype)


def steps_of(ncols):
    chips = ncols // 2
    steps = []
    for d in range(1, chips - 1, 2):
        steps += [(2 * d, 2 * d + 2), (2 * d + 2, 2 * d)]
    return steps + [(2 * chips - 2, 2 * chips - 2)] * (chips % 2 == 0 and chips > 1)


def body(left_query, left_value, right_key, right_value, bound):
    rows_n, width, depth = left_query.shape
    ncols = lax.axis_size("cols")
    here = lax.axis_index("cols")
    scale = 1.0 / math.sqrt(depth)

    def move(value, step):
        pairs = [(i, i ^ step[i % 2]) for i in range(ncols)]
        return lax.ppermute(value, "cols", pairs)

    def outgoing(step):
        up = source(*step) > here
        return jnp.stack((jnp.where(up, right_key, left_query), jnp.where(up, right_value, left_value)))

    steps = steps_of(ncols)
    near = [(move(outgoing(s), s), s) for s in steps]
    partner = move(outgoing((1, 1)), (1, 1))
    far = [(move(piece, (1, 1)), (s[1] ^ 1, s[0] ^ 1)) for piece, s in near]

    params = pltpu.CompilerParams(vmem_limit_bytes=16 * 1024 * 1024)
    flops = 4 * rows_n * width * width * depth
    state_shape = [
        jax.ShapeDtypeStruct((2, rows_n, width, 1), jnp.float32),
        jax.ShapeDtypeStruct((2, rows_n, width, 1), jnp.float32),
        jax.ShapeDtypeStruct((2, rows_n, width, depth), jnp.float32),
    ]
    mine, *state, bias = pl.pallas_call(
        functools.partial(own_kernel, scale),
        out_shape=[
            jax.ShapeDtypeStruct((2, rows_n, width, depth), jnp.bfloat16),
            *state_shape,
            jax.ShapeDtypeStruct((ncols, rows_n, 1, width), jnp.float32),
        ],
        in_specs=[SMEM] + [VMEM] * 4,
        out_specs=[VMEM] * 5,
        compiler_params=params,
        name="own",
    )(bound, left_query, left_value, right_key, right_value)

    def run(kernel, group, out_shape, aliases):
        pieces, offsets = zip(*group)
        return pl.pallas_call(
            functools.partial(kernel, offsets, scale),
            out_shape=out_shape,
            in_specs=[VMEM] * (5 + len(pieces)),
            out_specs=[VMEM] * len(out_shape),
            input_output_aliases=aliases,
            compiler_params=params,
            cost_estimate=pl.CostEstimate(
                flops=flops * len(pieces), bytes_accessed=(len(pieces) + 4) * 2**18, transcendentals=0
            ),
        )(bias, mine, *state, *pieces)

    groups = [[(partner, (1, 1))]]
    for i in range(0, len(steps) - 1, 2):
        groups += [[near[i], far[i + 1]], [near[i + 1], far[i]]]
    for group in groups:
        state = run(fold_kernel, group, state_shape, {2: 0, 3: 1, 4: 2})
    out = jax.ShapeDtypeStruct((rows_n, width, depth), jnp.bfloat16)
    return tuple(run(last_kernel, [near[-1], far[-1]], [out, out], {}))


def solution(mesh):
    spec = P("rows", "cols", None)

    return jax.shard_map(
        body,
        mesh=mesh,
        in_specs=(spec, spec, spec, spec, P("rows")),
        out_specs=(spec, spec),
        check_vma=False,
    )
```

profile of v0, /device:TPU:1, one launch (start us, length us, event | category | flops | bytes accessed | tf_op | source)
XLA Modules:
  0.0 23.7 jit_solution(11043518210108409884)
XLA Ops:
  0.7 1.2 %select_bitcast_fusion = (bf16[1,2,128,256]{3,2,1,0:T(8,128)(2,1)S(1)}, bf16[1,2,128,256]{3,2,1,0:T(8,128)(2,1)S(1)}, bf16[1,2,128,256]{3,2,1,0:T(8,128)(2,1)S(1...) fusion(bf16[2,128,256]{2,1,0:T(8,128)(2,1)} %rv_ref.1, ...), kind=kLoop, calls=%fused_computation.4 | loop fusion | flops 524288 | bytes 1572868 | tf_op jit(solution)/shard_map/stack | solution.py:112
  1.9 2.1 %collective-permute-start.2 = (bf16[2,2,128,256]{3,2,1,0:T(8,128)(2,1)S(1)}, bf16[2,2,128,256]{3,2,1,0:T(8,128)(2,1)S(1)}, u32[]{:S(2)}, u32[]{:S(2)}) collective-permute-start(bf16[2,2,128,256]{3,2,1,0:T(8,128)(2,1)S(1)} %pad_maximum_fusion.2), channel_id=1, source_target_pairs={{0,4},{1,3},{2,6},{3,1},{4,0},{5,7},{6,2},{7,5},{8,12},{9,11},{10,... | collective-permute-start | bytes 786440 | tf_op jit(solution)/shard_map/ppermute | solution.py:108
  4.0 1.3 %collective-permute-start.1 = (bf16[2,2,128,256]{3,2,1,0:T(8,128)(2,1)S(1)}, bf16[2,2,128,256]{3,2,1,0:T(8,128)(2,1)S(1)}, u32[]{:S(2)}, u32[]{:S(2)}) collective-permute-start(bf16[2,2,128,256]{3,2,1,0:T(8,128)(2,1)S(1)} %pad_maximum_fusion.1), channel_id=1, source_target_pairs={{0,2},{1,5},{2,0},{3,7},{4,6},{5,1},{6,4},{7,3},{8,10},{9,13},{10,... | collective-permute-start | bytes 786440 | tf_op jit(solution)/shard_map/ppermute | solution.py:108
  5.3 0.0 copy-start.4
  5.3 0.1 collective-permute-start.5
  5.4 0.0 copy-start
  5.4 0.0 copy-start.1
  5.4 0.0 copy-start.2
  5.4 0.0 copy-start.3
  5.5 1.3 %collective-permute-start = (bf16[2,2,128,256]{3,2,1,0:T(8,128)(2,1)S(1)}, bf16[2,2,128,256]{3,2,1,0:T(8,128)(2,1)S(1)}, u32[]{:S(2)}, u32[]{:S(2)}) collective-permute-start(bf16[2,2,128,256]{3,2,1,0:T(8,128)(2,1)S(1)} %pad_maximum_fusion), channel_id=1, source_target_pairs={{0,1},{1,0},{2,3},{3,2},{4,5},{5,4},{6,7},{7,6},{8,9},{9,8},{10,11... | collective-permute-start | bytes 786440 | tf_op jit(solution)/shard_map/ppermute | solution.py:108
  6.8 1.2 %collective-permute-done.2.rest_0_ = bf16[2,2,128,256]{3,2,1,0:T(8,128)(2,1)S(1)} collective-permute-done((bf16[2,2,128,256]{3,2,1,0:T(8,128)(2,1)S(1)}, bf16[2,2,128,256]{3,2,1,0:T(8,128)(2,1)S(1)}, u32[]{:S(2)}, u32[]{:S(2)}) %collective-permute-start.2) | collective-permute-done | bytes 262176 | tf_op jit(solution)/shard_map/ppermute | solution.py:108
  8.0 9.1 %collective-permute-start.3 = (bf16[2,2,128,256]{3,2,1,0:T(8,128)(2,1)S(1)}, bf16[2,2,128,256]{3,2,1,0:T(8,128)(2,1)S(1)}, u32[]{:S(2)}, u32[]{:S(2)}) collective-permute-start(bf16[2,2,128,256]{3,2,1,0:T(8,128)(2,1)S(1)} %collective-permute-done.2.rest_0_), channel_id=1, source_target_pairs={{0,1},{1,0},{2,3},{3,2},{4,5},{5,4},{6,7},{7,6},{8,9},{9,8},{10,11... | collective-permute-start | bytes 786440 | tf_op jit(solution)/shard_map/ppermute | solution.py:108
  17.1 0.0 collective-permute-done.1.rest_0_
  17.1 0.0 collective-permute-start.4
  17.1 0.0 collective-permute-done.5.rest_0_
  17.1 0.9 %collective-permute-start.6 = (bf16[2,2,128,256]{3,2,1,0:T(8,128)(2,1)S(1)}, bf16[2,2,128,256]{3,2,1,0:T(8,128)(2,1)S(1)}, u32[]{:S(2)}, u32[]{:S(2)}) collective-permute-start(bf16[2,2,128,256]{3,2,1,0:T(8,128)(2,1)S(1)} %collective-permute-done.5.rest_0_), channel_id=1, source_target_pairs={{0,1},{1,0},{2,3},{3,2},{4,5},{5,4},{6,7},{7,6},{8,9},{9,8},{10,11... | collective-permute-start | bytes 786440 | tf_op jit(solution)/shard_map/ppermute | solution.py:108
  18.0 0.0 copy-done.4
  18.0 0.0 copy-done
  18.0 0.0 copy-done.1
  18.1 0.0 copy-done.2
  18.1 0.0 copy-done.3
  18.1 1.2 %own.1 = (bf16[2,2,128,256]{3,2,1,0:T(8,128)(2,1)S(1)}, f32[2,2,128,1]{3,2,1,0:T(8,128)S(1)}, f32[2,2,128,1]{3,2,1,0:T(8,128)S(1)}, f32[2,2,128,256]{3,2,1,0:T(8,128)S(1)}, f32[8,2,1,128]{3,2,1,0:T(1,128)S(1)}) custom-call(s32[2]{0:T(128)S(1)} %copy-done.4, bf16[2,128,256]{2,1,0:T(8,128)(2,1)S(1)} %copy-done, bf16[2,128,256]{2,1,0:T(8,128)(2,1)S(1)} %copy-done.1, ...), custom_call_target="tpu_custom_call" | custom-call | tf_op jit(solution)/shard_map/own/pallas_call | solution.py:126
  19.3 0.0 collective-permute-done.rest_0_
  19.3 0.8 %shard_map.68 = (f32[2,2,128,1]{3,2,1,0:T(8,128)S(1)}, f32[2,2,128,1]{3,2,1,0:T(8,128)S(1)}, f32[2,2,128,256]{3,2,1,0:T(8,128)S(1)}) custom-call(f32[8,2,1,128]{3,2,1,0:T(1,128)S(1)} %get-tuple-element.16.bias, bf16[2,2,128,256]{3,2,1,0:T(8,128)(2,1)S(1)} %get-tuple-element.17.mine, ...), custom_call_target="tpu_custom_call", output_to_operand_aliasing={{0}: (2, {}), {1}: (3, {}), {2}: (4, {})} | custom-call | flops 33554432 | bytes 1310720 | tf_op jit(solution)/shard_map/pallas_call | solution.py:141
  20.1 0.0 collective-permute-done.3.rest_1_
  20.1 0.9 %shard_map.69 = (f32[2,2,128,1]{3,2,1,0:T(8,128)S(1)}, f32[2,2,128,1]{3,2,1,0:T(8,128)S(1)}, f32[2,2,128,256]{3,2,1,0:T(8,128)S(1)}) custom-call(f32[8,2,1,128]{3,2,1,0:T(1,128)S(1)} %get-tuple-element.16.bias, bf16[2,2,128,256]{3,2,1,0:T(8,128)(2,1)S(1)} %get-tuple-element.17.mine, ...), custom_call_target="tpu_custom_call", output_to_operand_aliasing={{0}: (2, {}), {1}: (3, {}), {2}: (4, {})} | custom-call | flops 67108864 | bytes 1572864 | tf_op jit(solution)/shard_map/pallas_call | solution.py:141
  21.0 0.0 collective-permute-done.4.rest_1_
  21.0 0.9 %shard_map.70 = (f32[2,2,128,1]{3,2,1,0:T(8,128)S(1)}, f32[2,2,128,1]{3,2,1,0:T(8,128)S(1)}, f32[2,2,128,256]{3,2,1,0:T(8,128)S(1)}) custom-call(f32[8,2,1,128]{3,2,1,0:T(1,128)S(1)} %get-tuple-element.16.bias, bf16[2,2,128,256]{3,2,1,0:T(8,128)(2,1)S(1)} %get-tuple-element.17.mine, ...), custom_call_target="tpu_custom_call", output_to_operand_aliasing={{0}: (2, {}), {1}: (3, {}), {2}: (4, {})} | custom-call | flops 67108864 | bytes 1572864 | tf_op jit(solution)/shard_map/pallas_call | solution.py:141
  21.9 0.0 collective-permute-done.6.rest_1_
  21.9 1.8 %shard_map.71 = (bf16[2,128,256]{2,1,0:T(8,128)(2,1)}, bf16[2,128,256]{2,1,0:T(8,128)(2,1)}) custom-call(f32[8,2,1,128]{3,2,1,0:T(1,128)S(1)} %get-tuple-element.16.bias, bf16[2,2,128,256]{3,2,1,0:T(8,128)(2,1)S(1)} %get-tuple-element.17.mine, f32[2,2,128,1]{3,2,1,0:T(8,128)S(1)} %get-tuple-element.27.top, f32[2,2,128,1]{3,2,1,0:T(8,128)S(1)} %get-tuple-element.28.total, ...), custom_call_target="tpu_custom_call" | custom-call | flops 67108864 | bytes 1572864 | tf_op jit(solution)/shard_map/pallas_call | solution.py:141
  (4 shorter events, 0.1 us)
Async XLA Ops:
  1.9 6.2 %collective-permute-start.2 = (bf16[2,2,128,256]{3,2,1,0:T(8,128)(2,1)S(1)}, bf16[2,2,128,256]{3,2,1,0:T(8,128)(2,1)S(1)}, u32[]{:S(2)}, u32[]{:S(2)}) collective-permute-start(bf16[2,2,128,256]{3,2,1,0:T(8,128)(2,1)S(1)} %pad_maximum_fusion.2), channel_id=1, source_target_pairs={{0,4},{1,3},{2,6},{3,1},{4,0},{5,7},{6,2},{7,5},{8,12},{9,11},{10,... | collective-permute-start | bytes 786440 | tf_op jit(solution)/shard_map/ppermute | solution.py:108
  4.0 13.1 %collective-permute-start.1 = (bf16[2,2,128,256]{3,2,1,0:T(8,128)(2,1)S(1)}, bf16[2,2,128,256]{3,2,1,0:T(8,128)(2,1)S(1)}, u32[]{:S(2)}, u32[]{:S(2)}) collective-permute-start(bf16[2,2,128,256]{3,2,1,0:T(8,128)(2,1)S(1)} %pad_maximum_fusion.1), channel_id=1, source_target_pairs={{0,2},{1,5},{2,0},{3,7},{4,6},{5,1},{6,4},{7,3},{8,10},{9,13},{10,... | collective-permute-start | bytes 786440 | tf_op jit(solution)/shard_map/ppermute | solution.py:108
  5.3 12.8 %copy-start.4 = (s32[2]{0:T(128)S(1)}, s32[2]{0:T(128)}, u32[]{:S(2)}) copy-start(s32[2]{0:T(128)} %bound_ref.1) | copy-start | bytes 28
  5.3 11.8 %collective-permute-start.5 = (bf16[2,2,128,256]{3,2,1,0:T(8,128)(2,1)S(1)}, bf16[2,2,128,256]{3,2,1,0:T(8,128)(2,1)S(1)}, u32[]{:S(2)}, u32[]{:S(2)}) collective-permute-start(bf16[2,2,128,256]{3,2,1,0:T(8,128)(2,1)S(1)} %pad_maximum_fusion.3), channel_id=1, source_target_pairs={{0,6},{1,7},{2,4},{3,5},{4,2},{5,3},{6,0},{7,1},{8,14},{9,15},{10,... | collective-permute-start | bytes 786440 | tf_op jit(solution)/shard_map/ppermute | solution.py:108
  5.4 12.6 %copy-start = (bf16[2,128,256]{2,1,0:T(8,128)(2,1)S(1)}, bf16[2,128,256]{2,1,0:T(8,128)(2,1)}, u32[]{:S(2)}) copy-start(bf16[2,128,256]{2,1,0:T(8,128)(2,1)} %q_ref.1) | copy-start | bytes 393220
  5.4 12.6 %copy-start.1 = (bf16[2,128,256]{2,1,0:T(8,128)(2,1)S(1)}, bf16[2,128,256]{2,1,0:T(8,128)(2,1)}, u32[]{:S(2)}) copy-start(bf16[2,128,256]{2,1,0:T(8,128)(2,1)} %lv_ref.1) | copy-start | bytes 393220
  5.4 12.6 %copy-start.2 = (bf16[2,128,256]{2,1,0:T(8,128)(2,1)S(1)}, bf16[2,128,256]{2,1,0:T(8,128)(2,1)}, u32[]{:S(2)}) copy-start(bf16[2,128,256]{2,1,0:T(8,128)(2,1)} %k_ref.1) | copy-start | bytes 393220
  5.4 12.6 %copy-start.3 = (bf16[2,128,256]{2,1,0:T(8,128)(2,1)S(1)}, bf16[2,128,256]{2,1,0:T(8,128)(2,1)}, u32[]{:S(2)}) copy-start(bf16[2,128,256]{2,1,0:T(8,128)(2,1)} %rv_ref.1) | copy-start | bytes 393220
  5.5 13.8 %collective-permute-start = (bf16[2,2,128,256]{3,2,1,0:T(8,128)(2,1)S(1)}, bf16[2,2,128,256]{3,2,1,0:T(8,128)(2,1)S(1)}, u32[]{:S(2)}, u32[]{:S(2)}) collective-permute-start(bf16[2,2,128,256]{3,2,1,0:T(8,128)(2,1)S(1)} %pad_maximum_fusion), channel_id=1, source_target_pairs={{0,1},{1,0},{2,3},{3,2},{4,5},{5,4},{6,7},{7,6},{8,9},{9,8},{10,11... | collective-permute-start | bytes 786440 | tf_op jit(solution)/shard_map/ppermute | solution.py:108
  8.0 12.1 %collective-permute-start.3 = (bf16[2,2,128,256]{3,2,1,0:T(8,128)(2,1)S(1)}, bf16[2,2,128,256]{3,2,1,0:T(8,128)(2,1)S(1)}, u32[]{:S(2)}, u32[]{:S(2)}) collective-permute-start(bf16[2,2,128,256]{3,2,1,0:T(8,128)(2,1)S(1)} %collective-permute-done.2.rest_0_), channel_id=1, source_target_pairs={{0,1},{1,0},{2,3},{3,2},{4,5},{5,4},{6,7},{7,6},{8,9},{9,8},{10,11... | collective-permute-start | bytes 786440 | tf_op jit(solution)/shard_map/ppermute | solution.py:108
  17.1 3.9 %collective-permute-start.4 = (bf16[2,2,128,256]{3,2,1,0:T(8,128)(2,1)S(1)}, bf16[2,2,128,256]{3,2,1,0:T(8,128)(2,1)S(1)}, u32[]{:S(2)}, u32[]{:S(2)}) collective-permute-start(bf16[2,2,128,256]{3,2,1,0:T(8,128)(2,1)S(1)} %collective-permute-done.1.rest_0_), channel_id=1, source_target_pairs={{0,1},{1,0},{2,3},{3,2},{4,5},{5,4},{6,7},{7,6},{8,9},{9,8},{10,11... | collective-permute-start | bytes 786440 | tf_op jit(solution)/shard_map/ppermute | solution.py:108
  17.1 4.8 %collective-permute-start.6 = (bf16[2,2,128,256]{3,2,1,0:T(8,128)(2,1)S(1)}, bf16[2,2,128,256]{3,2,1,0:T(8,128)(2,1)S(1)}, u32[]{:S(2)}, u32[]{:S(2)}) collective-permute-start(bf16[2,2,128,256]{3,2,1,0:T(8,128)(2,1)S(1)} %collective-permute-done.5.rest_0_), channel_id=1, source_target_pairs={{0,1},{1,0},{2,3},{3,2},{4,5},{5,4},{6,7},{7,6},{8,9},{9,8},{10,11... | collective-permute-start | bytes 786440 | tf_op jit(solution)/shard_map/ppermute | solution.py:108
where the time goes:
time: 23.9 us; the launch traced here: 23.7 us
  starting transfers between devices  14.8 us (62%)
  Pallas kernels  5.58 us (23%)
  other arithmetic  1.28 us (5%)
  waiting for transfers between devices  1.24 us (5%)
  between operations  0.79 us (3%)
    ppermute x7, starting transfers between devices, move(): return lax.ppermute(value, 'cols', pairs)  14.8 us
    pallas_call x4, Pallas kernels, run(): pl.pallas_call(functools.partial(kernel, offsets, scale), out_shape=out_s...  4.35 us
    another operation x5, other arithmetic, outgoing(): jnp.stack((jnp.where(up, right_key, left_query), jnp.where(up, right_valu...  1.28 us
    ppermute x7, waiting for transfers between devices, move(): return lax.ppermute(value, 'cols', pairs)  1.24 us
    pallas_call x1, Pallas kernels, body(): pl.pallas_call(functools.partial(own_kernel, scale), out_shape=[jax.Shape...  1.23 us
  transfers between devices with their start and end apart: 7, of which 1 were waited for; matrix products, arithmetic and copies ran while one was open for 0% of the time, Pallas kernels for 16%

commit v1 on v0

--- a/solution.py
+++ b/solution.py
@@ -36,10 +36,10 @@
         for r in range(rows_n):
             mine[side, r] = a_ref[r]
             s = jnp.where(valid, scores(a_ref[r], b_ref[r], scale), LOW)
-            m = jnp.max(s, axis=-1, keepdims=True)
+            m = jnp.broadcast_to(jnp.max(s, axis=-1, keepdims=True), s.shape)
             w = jnp.exp(s - m)
             top[side, r] = m
-            total[side, r] = jnp.sum(w, axis=-1, keepdims=True)
+            total[side, r] = w
             acc[side, r] = weighted(w, v_ref[r])
 
 
@@ -60,15 +60,14 @@
             for (piece, _), other in zip(group, others)
         ]
         old = top[side, r]
-        m = old
-        for s in parts:
-            m = jnp.maximum(m, jnp.max(s, axis=-1, keepdims=True))
+        peak = functools.reduce(jnp.maximum, parts)
+        m = jnp.maximum(old, jnp.max(peak, axis=-1, keepdims=True))
         factor = jnp.exp(old - m)
         summed = total[side, r] * factor
-        product = acc[side, r] * factor
+        product = acc[side, r] * jnp.concatenate([factor] * (acc.shape[-1] // factor.shape[-1]), axis=-1)
         for s, (piece, _) in zip(parts, group):
             w = jnp.exp(s - m)
-            summed = summed + jnp.sum(w, axis=-1, keepdims=True)
+            summed = summed + w
             product = product + weighted(w, piece[1, r])
         new_top[side, r] = m
         new_total[side, r] = summed
@@ -86,7 +85,8 @@
     fold(scale, bias, mine, state, state, list(zip(pieces, steps)))
     for side, out in enumerate((left_ref, right_ref)):
         for r in range(out.shape[0]):
-            out[r] = (acc[side, r] / total[side, r]).astype(out.dtype)
+            inverse = 1.0 / jnp.sum(total[side, r], axis=-1, keepdims=True)
+            out[r] = (acc[side, r] * inverse).astype(out.dtype)
 
 
 def steps_of(ncols):
@@ -100,7 +100,6 @@
 def body(left_query, left_value, right_key, right_value, bound):
     rows_n, width, depth = left_query.shape
     ncols = lax.axis_size("cols")
-    here = lax.axis_index("cols")
     scale = 1.0 / math.sqrt(depth)
 
     def move(value, step):
@@ -108,19 +107,19 @@
         return lax.ppermute(value, "cols", pairs)
 
     def outgoing(step):
-        up = source(*step) > here
+        up = source(*step) > lax.axis_index("cols")
         return jnp.stack((jnp.where(up, right_key, left_query), jnp.where(up, right_value, left_value)))
 
+    params = pltpu.CompilerParams(vmem_limit_bytes=16 * 1024 * 1024)
     steps = steps_of(ncols)
     near = [(move(outgoing(s), s), s) for s in steps]
     partner = move(outgoing((1, 1)), (1, 1))
     far = [(move(piece, (1, 1)), (s[1] ^ 1, s[0] ^ 1)) for piece, s in near]
 
-    params = pltpu.CompilerParams(vmem_limit_bytes=16 * 1024 * 1024)
     flops = 4 * rows_n * width * width * depth
     state_shape = [
-        jax.ShapeDtypeStruct((2, rows_n, width, 1), jnp.float32),
-        jax.ShapeDtypeStruct((2, rows_n, width, 1), jnp.float32),
+        jax.ShapeDtypeStruct((2, rows_n, width, width), jnp.float32),
+        jax.ShapeDtypeStruct((2, rows_n, width, width), jnp.float32),
         jax.ShapeDtypeStruct((2, rows_n, width, depth), jnp.float32),
     ]
     mine, *state, bias = pl.pallas_call(
@@ -153,10 +152,11 @@
     groups = [[(partner, (1, 1))]]
     for i in range(0, len(steps) - 1, 2):
         groups += [[near[i], far[i + 1]], [near[i + 1], far[i]]]
+    groups += [[near[-1]]]
     for group in groups:
         state = run(fold_kernel, group, state_shape, {2: 0, 3: 1, 4: 2})
     out = jax.ShapeDtypeStruct((rows_n, width, depth), jnp.bfloat16)
-    return tuple(run(last_kernel, [near[-1], far[-1]], [out, out], {}))
+    return tuple(run(last_kernel, [far[-1]], [out, out], {}))
 
 
 def solution(mesh):

time: 23.9 us -> 23.4 us (0.979)
  Pallas kernels: 5.58 us -> 5.13 us
    pallas_call x4 -> x5, Pallas kernels: 4.35 us -> 3.9 us  [run(): pl.pallas_call(functools.partial(kernel, offsets, scale), out_shape=out_s...]
where the time goes in v1:
time: 23.4 us; the launch traced here: 23.3 us
  starting transfers between devices  14.8 us (63%)
  Pallas kernels  5.13 us (22%)
  other arithmetic  1.28 us (5%)
  waiting for transfers between devices  1.24 us (5%)
  between operations  0.8 us (3%)
    ppermute x7, starting transfers between devices, move(): return lax.ppermute(value, 'cols', pairs)  14.8 us
    pallas_call x5, Pallas kernels, run(): pl.pallas_call(functools.partial(kernel, offsets, scale), out_shape=out_s...  3.9 us
    another operation x5, other arithmetic, outgoing(): jnp.stack((jnp.where(up, right_key, left_query), jnp.where(up, right_valu...  1.28 us
    ppermute x7, waiting for transfers between devices, move(): return lax.ppermute(value, 'cols', pairs)  1.24 us
    pallas_call x1, Pallas kernels, body(): pl.pallas_call(functools.partial(own_kernel, scale), out_shape=[jax.Shape...  1.23 us
  transfers between devices with their start and end apart: 7, of which 1 were waited for; matrix products, arithmetic and copies ran while one was open for 0% of the time, Pallas kernels for 16%

profile of v1, /device:TPU:1, one launch (start us, length us, event | category | flops | bytes accessed | tf_op | source)
XLA Modules:
  0.0 23.3 jit_solution(5191906992202188624)
XLA Ops:
  0.7 1.2 %select_bitcast_fusion = (bf16[1,2,128,256]{3,2,1,0:T(8,128)(2,1)S(1)}, bf16[1,2,128,256]{3,2,1,0:T(8,128)(2,1)S(1)}, bf16[1,2,128,256]{3,2,1,0:T(8,128)(2,1)S(1...) fusion(bf16[2,128,256]{2,1,0:T(8,128)(2,1)} %rv_ref.1, ...), kind=kLoop, calls=%fused_computation.4 | loop fusion | flops 524288 | bytes 1572868 | tf_op jit(solution)/shard_map/stack | solution.py:111
  1.9 2.1 %collective-permute-start.2 = (bf16[2,2,128,256]{3,2,1,0:T(8,128)(2,1)S(1)}, bf16[2,2,128,256]{3,2,1,0:T(8,128)(2,1)S(1)}, u32[]{:S(2)}, u32[]{:S(2)}) collective-permute-start(bf16[2,2,128,256]{3,2,1,0:T(8,128)(2,1)S(1)} %pad_maximum_fusion.2), channel_id=1, source_target_pairs={{0,4},{1,3},{2,6},{3,1},{4,0},{5,7},{6,2},{7,5},{8,12},{9,11},{10,... | collective-permute-start | bytes 786440 | tf_op jit(solution)/shard_map/ppermute | solution.py:107
  4.0 1.3 %collective-permute-start.1 = (bf16[2,2,128,256]{3,2,1,0:T(8,128)(2,1)S(1)}, bf16[2,2,128,256]{3,2,1,0:T(8,128)(2,1)S(1)}, u32[]{:S(2)}, u32[]{:S(2)}) collective-permute-start(bf16[2,2,128,256]{3,2,1,0:T(8,128)(2,1)S(1)} %pad_maximum_fusion.1), channel_id=1, source_target_pairs={{0,2},{1,5},{2,0},{3,7},{4,6},{5,1},{6,4},{7,3},{8,10},{9,13},{10,... | collective-permute-start | bytes 786440 | tf_op jit(solution)/shard_map/ppermute | solution.py:107
  5.3 0.0 copy-start.4
  5.3 0.1 collective-permute-start.5
  5.4 0.0 copy-start
  5.4 0.0 copy-start.1
  5.4 0.0 copy-start.2
  5.4 0.0 copy-start.3
  5.5 1.3 %collective-permute-start = (bf16[2,2,128,256]{3,2,1,0:T(8,128)(2,1)S(1)}, bf16[2,2,128,256]{3,2,1,0:T(8,128)(2,1)S(1)}, u32[]{:S(2)}, u32[]{:S(2)}) collective-permute-start(bf16[2,2,128,256]{3,2,1,0:T(8,128)(2,1)S(1)} %pad_maximum_fusion), channel_id=1, source_target_pairs={{0,1},{1,0},{2,3},{3,2},{4,5},{5,4},{6,7},{7,6},{8,9},{9,8},{10,11... | collective-permute-start | bytes 786440 | tf_op jit(solution)/shard_map/ppermute | solution.py:107
  6.8 1.2 %collective-permute-done.2.rest_0_ = bf16[2,2,128,256]{3,2,1,0:T(8,128)(2,1)S(1)} collective-permute-done((bf16[2,2,128,256]{3,2,1,0:T(8,128)(2,1)S(1)}, bf16[2,2,128,256]{3,2,1,0:T(8,128)(2,1)S(1)}, u32[]{:S(2)}, u32[]{:S(2)}) %collective-permute-start.2) | collective-permute-done | bytes 262176 | tf_op jit(solution)/shard_map/ppermute | solution.py:107
  8.0 9.1 %collective-permute-start.3 = (bf16[2,2,128,256]{3,2,1,0:T(8,128)(2,1)S(1)}, bf16[2,2,128,256]{3,2,1,0:T(8,128)(2,1)S(1)}, u32[]{:S(2)}, u32[]{:S(2)}) collective-permute-start(bf16[2,2,128,256]{3,2,1,0:T(8,128)(2,1)S(1)} %collective-permute-done.2.rest_0_), channel_id=1, source_target_pairs={{0,1},{1,0},{2,3},{3,2},{4,5},{5,4},{6,7},{7,6},{8,9},{9,8},{10,11... | collective-permute-start | bytes 786440 | tf_op jit(solution)/shard_map/ppermute | solution.py:107
  17.1 0.0 collective-permute-done.1.rest_0_
  17.1 0.0 collective-permute-start.4
  17.1 0.0 collective-permute-done.5.rest_0_
  17.1 0.9 %collective-permute-start.6 = (bf16[2,2,128,256]{3,2,1,0:T(8,128)(2,1)S(1)}, bf16[2,2,128,256]{3,2,1,0:T(8,128)(2,1)S(1)}, u32[]{:S(2)}, u32[]{:S(2)}) collective-permute-start(bf16[2,2,128,256]{3,2,1,0:T(8,128)(2,1)S(1)} %collective-permute-done.5.rest_0_), channel_id=1, source_target_pairs={{0,1},{1,0},{2,3},{3,2},{4,5},{5,4},{6,7},{7,6},{8,9},{9,8},{10,11... | collective-permute-start | bytes 786440 | tf_op jit(solution)/shard_map/ppermute | solution.py:107
  18.0 0.0 copy-done.4
  18.0 0.0 copy-done
  18.0 0.0 copy-done.1
  18.1 0.0 copy-done.2
  18.1 0.0 copy-done.3
  18.1 1.2 %own.1 = (bf16[2,2,128,256]{3,2,1,0:T(8,128)(2,1)S(1)}, f32[2,2,128,128]{3,2,1,0:T(8,128)S(1)}, f32[2,2,128,128]{3,2,1,0:T(8,128)S(1)}, f32[2,2,128,256]{3,2,1,0:T(8,128)S(1)}, f32[8,2,1,128]{3,2,1,0:T(1,128)S(1)}) custom-call(s32[2]{0:T(128)S(1)} %copy-done.4, bf16[2,128,256]{2,1,0:T(8,128)(2,1)S(1)} %copy-done, bf16[2,128,256]{2,1,0:T(8,128)(2,1)S(1)} %copy-done.1, ...), custom_call_target="tpu_custom_call" | custom-call | tf_op jit(solution)/shard_map/own/pallas_call | solution.py:125
  19.3 0.0 collective-permute-done.rest_0_
  19.3 0.7 %shard_map.68 = (f32[2,2,128,128]{3,2,1,0:T(8,128)S(1)}, f32[2,2,128,128]{3,2,1,0:T(8,128)S(1)}, f32[2,2,128,256]{3,2,1,0:T(8,128)S(1)}) custom-call(f32[8,2,1,128]{3,2,1,0:T(1,128)S(1)} %get-tuple-element.19.bias, bf16[2,2,128,256]{3,2,1,0:T(8,128)(2,1)S(1)} %get-tuple-element.20.mine, ...), custom_call_target="tpu_custom_call", output_to_operand_aliasing={{0}: (2, {}), {1}: (3, {}), {2}: (4, {})} | custom-call | flops 33554432 | bytes 1310720 | tf_op jit(solution)/shard_map/pallas_call | solution.py:140
  20.0 0.0 collective-permute-done.3.rest_1_
  20.0 0.6 %shard_map.69 = (f32[2,2,128,128]{3,2,1,0:T(8,128)S(1)}, f32[2,2,128,128]{3,2,1,0:T(8,128)S(1)}, f32[2,2,128,256]{3,2,1,0:T(8,128)S(1)}) custom-call(f32[8,2,1,128]{3,2,1,0:T(1,128)S(1)} %get-tuple-element.19.bias, bf16[2,2,128,256]{3,2,1,0:T(8,128)(2,1)S(1)} %get-tuple-element.20.mine, ...), custom_call_target="tpu_custom_call", output_to_operand_aliasing={{0}: (2, {}), {1}: (3, {}), {2}: (4, {})} | custom-call | flops 67108864 | bytes 1572864 | tf_op jit(solution)/shard_map/pallas_call | solution.py:140
  20.6 0.0 collective-permute-done.4.rest_1_
  20.6 0.6 %shard_map.70 = (f32[2,2,128,128]{3,2,1,0:T(8,128)S(1)}, f32[2,2,128,128]{3,2,1,0:T(8,128)S(1)}, f32[2,2,128,256]{3,2,1,0:T(8,128)S(1)}) custom-call(f32[8,2,1,128]{3,2,1,0:T(1,128)S(1)} %get-tuple-element.19.bias, bf16[2,2,128,256]{3,2,1,0:T(8,128)(2,1)S(1)} %get-tuple-element.20.mine, ...), custom_call_target="tpu_custom_call", output_to_operand_aliasing={{0}: (2, {}), {1}: (3, {}), {2}: (4, {})} | custom-call | flops 67108864 | bytes 1572864 | tf_op jit(solution)/shard_map/pallas_call | solution.py:140
  21.2 0.7 %shard_map.71 = (f32[2,2,128,128]{3,2,1,0:T(8,128)S(1)}, f32[2,2,128,128]{3,2,1,0:T(8,128)S(1)}, f32[2,2,128,256]{3,2,1,0:T(8,128)S(1)}) custom-call(f32[8,2,1,128]{3,2,1,0:T(1,128)S(1)} %get-tuple-element.19.bias, bf16[2,2,128,256]{3,2,1,0:T(8,128)(2,1)S(1)} %get-tuple-element.20.mine, ...), custom_call_target="tpu_custom_call", output_to_operand_aliasing={{0}: (2, {}), {1}: (3, {}), {2}: (4, {})} | custom-call | flops 33554432 | bytes 1310720 | tf_op jit(solution)/shard_map/pallas_call | solution.py:140
  21.9 0.0 collective-permute-done.6.rest_0_
  21.9 1.4 %shard_map.72 = (bf16[2,128,256]{2,1,0:T(8,128)(2,1)}, bf16[2,128,256]{2,1,0:T(8,128)(2,1)}) custom-call(f32[8,2,1,128]{3,2,1,0:T(1,128)S(1)} %get-tuple-element.19.bias, bf16[2,2,128,256]{3,2,1,0:T(8,128)(2,1)S(1)} %get-tuple-element.20.mine, f32[2,2,128,128]{3,2,1,0:T(8,128)S(1)} %get-tuple-element.33.top, f32[2,2,128,128]{3,2,1,0:T(8,128)S(1)} %get-tuple-element.34.total, ...), custom_call_target="tpu_custom_call" | custom-call | flops 33554432 | bytes 1310720 | tf_op jit(solution)/shard_map/pallas_call | solution.py:140
  (4 shorter events, 0.1 us)
Async XLA Ops:
  1.9 6.2 %collective-permute-start.2 = (bf16[2,2,128,256]{3,2,1,0:T(8,128)(2,1)S(1)}, bf16[2,2,128,256]{3,2,1,0:T(8,128)(2,1)S(1)}, u32[]{:S(2)}, u32[]{:S(2)}) collective-permute-start(bf16[2,2,128,256]{3,2,1,0:T(8,128)(2,1)S(1)} %pad_maximum_fusion.2), channel_id=1, source_target_pairs={{0,4},{1,3},{2,6},{3,1},{4,0},{5,7},{6,2},{7,5},{8,12},{9,11},{10,... | collective-permute-start | bytes 786440 | tf_op jit(solution)/shard_map/ppermute | solution.py:107
  4.0 13.1 %collective-permute-start.1 = (bf16[2,2,128,256]{3,2,1,0:T(8,128)(2,1)S(1)}, bf16[2,2,128,256]{3,2,1,0:T(8,128)(2,1)S(1)}, u32[]{:S(2)}, u32[]{:S(2)}) collective-permute-start(bf16[2,2,128,256]{3,2,1,0:T(8,128)(2,1)S(1)} %pad_maximum_fusion.1), channel_id=1, source_target_pairs={{0,2},{1,5},{2,0},{3,7},{4,6},{5,1},{6,4},{7,3},{8,10},{9,13},{10,... | collective-permute-start | bytes 786440 | tf_op jit(solution)/shard_map/ppermute | solution.py:107
  5.3 12.8 %copy-start.4 = (s32[2]{0:T(128)S(1)}, s32[2]{0:T(128)}, u32[]{:S(2)}) copy-start(s32[2]{0:T(128)} %bound_ref.1) | copy-start | bytes 28
  5.3 11.8 %collective-permute-start.5 = (bf16[2,2,128,256]{3,2,1,0:T(8,128)(2,1)S(1)}, bf16[2,2,128,256]{3,2,1,0:T(8,128)(2,1)S(1)}, u32[]{:S(2)}, u32[]{:S(2)}) collective-permute-start(bf16[2,2,128,256]{3,2,1,0:T(8,128)(2,1)S(1)} %pad_maximum_fusion.3), channel_id=1, source_target_pairs={{0,6},{1,7},{2,4},{3,5},{4,2},{5,3},{6,0},{7,1},{8,14},{9,15},{10,... | collective-permute-start | bytes 786440 | tf_op jit(solution)/shard_map/ppermute | solution.py:107
  5.4 12.6 %copy-start = (bf16[2,128,256]{2,1,0:T(8,128)(2,1)S(1)}, bf16[2,128,256]{2,1,0:T(8,128)(2,1)}, u32[]{:S(2)}) copy-start(bf16[2,128,256]{2,1,0:T(8,128)(2,1)} %q_ref.1) | copy-start | bytes 393220
  5.4 12.6 %copy-start.1 = (bf16[2,128,256]{2,1,0:T(8,128)(2,1)S(1)}, bf16[2,128,256]{2,1,0:T(8,128)(2,1)}, u32[]{:S(2)}) copy-start(bf16[2,128,256]{2,1,0:T(8,128)(2,1)} %lv_ref.1) | copy-start | bytes 393220
  5.4 12.6 %copy-start.2 = (bf16[2,128,256]{2,1,0:T(8,128)(2,1)S(1)}, bf16[2,128,256]{2,1,0:T(8,128)(2,1)}, u32[]{:S(2)}) copy-start(bf16[2,128,256]{2,1,0:T(8,128)(2,1)} %k_ref.1) | copy-start | bytes 393220
  5.4 12.6 %copy-start.3 = (bf16[2,128,256]{2,1,0:T(8,128)(2,1)S(1)}, bf16[2,128,256]{2,1,0:T(8,128)(2,1)}, u32[]{:S(2)}) copy-start(bf16[2,128,256]{2,1,0:T(8,128)(2,1)} %rv_ref.1) | copy-start | bytes 393220
  5.5 13.8 %collective-permute-start = (bf16[2,2,128,256]{3,2,1,0:T(8,128)(2,1)S(1)}, bf16[2,2,128,256]{3,2,1,0:T(8,128)(2,1)S(1)}, u32[]{:S(2)}, u32[]{:S(2)}) collective-permute-start(bf16[2,2,128,256]{3,2,1,0:T(8,128)(2,1)S(1)} %pad_maximum_fusion), channel_id=1, source_target_pairs={{0,1},{1,0},{2,3},{3,2},{4,5},{5,4},{6,7},{7,6},{8,9},{9,8},{10,11... | collective-permute-start | bytes 786440 | tf_op jit(solution)/shard_map/ppermute | solution.py:107
  8.0 12.0 %collective-permute-start.3 = (bf16[2,2,128,256]{3,2,1,0:T(8,128)(2,1)S(1)}, bf16[2,2,128,256]{3,2,1,0:T(8,128)(2,1)S(1)}, u32[]{:S(2)}, u32[]{:S(2)}) collective-permute-start(bf16[2,2,128,256]{3,2,1,0:T(8,128)(2,1)S(1)} %collective-permute-done.2.rest_0_), channel_id=1, source_target_pairs={{0,1},{1,0},{2,3},{3,2},{4,5},{5,4},{6,7},{7,6},{8,9},{9,8},{10,11... | collective-permute-start | bytes 786440 | tf_op jit(solution)/shard_map/ppermute | solution.py:107
  17.1 3.5 %collective-permute-start.4 = (bf16[2,2,128,256]{3,2,1,0:T(8,128)(2,1)S(1)}, bf16[2,2,128,256]{3,2,1,0:T(8,128)(2,1)S(1)}, u32[]{:S(2)}, u32[]{:S(2)}) collective-permute-start(bf16[2,2,128,256]{3,2,1,0:T(8,128)(2,1)S(1)} %collective-permute-done.1.rest_0_), channel_id=1, source_target_pairs={{0,1},{1,0},{2,3},{3,2},{4,5},{5,4},{6,7},{7,6},{8,9},{9,8},{10,11... | collective-permute-start | bytes 786440 | tf_op jit(solution)/shard_map/ppermute | solution.py:107
  17.1 4.8 %collective-permute-start.6 = (bf16[2,2,128,256]{3,2,1,0:T(8,128)(2,1)S(1)}, bf16[2,2,128,256]{3,2,1,0:T(8,128)(2,1)S(1)}, u32[]{:S(2)}, u32[]{:S(2)}) collective-permute-start(bf16[2,2,128,256]{3,2,1,0:T(8,128)(2,1)S(1)} %collective-permute-done.5.rest_0_), channel_id=1, source_target_pairs={{0,1},{1,0},{2,3},{3,2},{4,5},{5,4},{6,7},{7,6},{8,9},{9,8},{10,11... | collective-permute-start | bytes 786440 | tf_op jit(solution)/shard_map/ppermute | solution.py:107
